TPU v7x, 512 devices: a whole 4x4x16 slice. The times are simulated.
512 devices in a mesh: gx: 32 (over x, y, core), gy: 16 (over z).
Axes of the slice: x: 4, y: 4, z: 16, core: 2. Of those that a mesh axis runs over, the one named last changes fastest.
Arguments:
- schur_blocks: float32 [32, 16, 768, 768], P('gx', 'gy'), may hold values from -32 to 32, as said below
- basis: float32 [32, 16, 32, 768], P('gx', 'gy'), may hold values from -0.21875 to 0.21875
- loads: float32 [32, 16, 16, 768], P('gx', 'gy'), may hold values from -64 to 64
- coarse_inverse: float32 [16384, 16384], P(('gx', 'gy')), may hold values from -0.09375 to 0.09375
- iface_map: int32 [32, 16, 768], P('gx', 'gy'), may hold values from 0 to 767, as said below
- coarse_slot: int32 [512], replicated, may hold values from 0 to 511, each once
Outputs:
- solution: float32 [32, 16, 16, 768], P('gx', 'gy')
Inputs may be any that keep to these rules, and one draw needn't show every extreme that they name: `schur_blocks`: each block is symmetric. `iface_map`: for every subdomain the map is a permutation of 0 to 767 that maps each aligned block of 128 cells onto itself. `coarse_slot`: every subdomain has its own coarse block number.
All inputs are finite; a program needn't handle non-finite values.
Results may differ from a plain program's by a relative error of at most 0.0001.
Values sent between devices are 32-bit elements; how exact they have to be, the bound alone decides.
No kernel may reach another device: no remote copies, remote signals or barrier semaphores. Data moves between devices by JAX's collectives and lax.ppermute only.
A program may use at most 128 MiB of HBM per device.

v0:
```python
import jax
import jax.numpy as jnp
from jax import lax
from jax.sharding import PartitionSpec as P

EW = 256
ES = 128
ITERS = 3
highest = lax.Precision.HIGHEST
epsilon = 1e-06


def padded(block, sides, width):
    for axis, dim in sides:
        count = lax.axis_size(axis)
        forward = [(i, i + 1) for i in range(count - 1)]
        backward = [(target, source) for source, target in forward]
        low = lax.ppermute(
            lax.slice_in_dim(block, block.shape[dim] - width, None, axis=dim), axis, forward
        )
        high = lax.ppermute(lax.slice_in_dim(block, 0, width, axis=dim), axis, backward)
        block = jnp.concatenate([low, block, high], axis=dim)
    return block


def edge_stacks(layout):
    column_edges = jnp.stack([layout[:, :EW], layout[:, EW : 2 * EW]])
    row_edges = jnp.stack([layout[:, 2 * EW : 2 * EW + ES], layout[:, 2 * EW + ES :]])
    return (column_edges, row_edges)


def add_edges(values, position, across, along):
    outside = jnp.concatenate([across[0], across[3], along[0], along[3]], axis=1)
    return values + jnp.take(outside, position, axis=1)


def assemble(values, position, inverse):
    column_edges, row_edges = edge_stacks(jnp.take(values, inverse, axis=1))
    across = padded(column_edges, (("gy", 0),), 1)
    along = padded(row_edges, (("gx", 0),), 1)
    return add_edges(values, position, across, along)


def per_device(schur_blocks, basis, loads, coarse_inverse, iface_map, coarse_slot):
    schur_block = schur_blocks[0, 0]
    local_basis = basis[0, 0]
    position = iface_map[0, 0]
    inverse = jnp.argsort(position)
    mode_count = local_basis.shape[0]
    domain_count = coarse_slot.shape[0]
    reordered = jnp.take(
        coarse_inverse.reshape(mode_count, domain_count, mode_count), coarse_slot, axis=1
    )
    reordered = reordered.reshape(mode_count, domain_count * mode_count)
    residual = assemble(loads[0, 0], position, inverse)
    solution = jnp.zeros_like(residual)
    for iteration in range(ITERS):
        lifted = lax.dot_general(
            lax.all_gather(
                lax.dot_general(
                    residual,
                    local_basis,
                    (((1,), (1,)), ((), ())),
                    precision=highest,
                    preferred_element_type=jnp.float32,
                ),
                ("gx", "gy"),
                axis=1,
                tiled=True,
            ),
            reordered,
            (((1,), (1,)), ((), ())),
            precision=highest,
            preferred_element_type=jnp.float32,
        )
        spread = jnp.dot(lifted, local_basis, precision=highest, preferred_element_type=jnp.float32)
        column_edges, row_edges = edge_stacks(jnp.take(spread, inverse, axis=1))
        across = padded(column_edges, (("gy", 0),), 1)
        along = padded(row_edges, (("gx", 0),), 1)
        search = residual + add_edges(spread, position, across, along)
        local_image = jnp.dot(
            search, schur_block, precision=highest, preferred_element_type=jnp.float32
        )
        applied = assemble(local_image, position, inverse)
        totals = lax.psum(
            (jnp.sum(residual * applied, axis=1), jnp.sum(applied * applied, axis=1)), ("gx", "gy")
        )
        stride = (totals[0] / (totals[1] + epsilon))[:, None]
        solution = solution + stride * search
        residual = residual - stride * applied
    return solution[None, None]


def solution(mesh):
    placed = (
        P("gx", "gy", None, None),
        P("gx", "gy", None, None),
        P("gx", "gy", None, None),
        P(("gx", "gy"), None),
        P("gx", "gy", None),
        P(),
    )
    return jax.shard_map(
        per_device, mesh=mesh, in_specs=placed, out_specs=P("gx", "gy", None, None), check_vma=False
    )
```

profile of v0, /device:TPU:1, one launch (start us, length us, event | category | flops | bytes accessed | tf_op | source)
XLA Modules:
  0.0 1102.9 jit_solution(14531170180641245100)
XLA Ops:
  7.4 4.4 sort.17
  14.6 4.4 collective-permute-start
  20.3 4.0 collective-permute-start.2
  24.3 2.9 collective-permute-start.3
  27.3 2.6 collective-permute-done.3
  32.6 6.4 reshape.19
  39.0 11.5 %copy.97 = f32[32,512,32]{2,0,1:T(8,128)} copy(f32[32,512,32]{2,1,0:T(8,128)} %reshape.19) | data formatting | bytes 4194304 | tf_op jit(solution)/shard_map/reshape | solution.py:52
  50.5 7.7 gather_fusion
  58.3 11.5 %copy.98 = f32[32,512,32]{2,1,0:T(8,128)} copy(f32[32,512,32]{2,0,1:T(8,128)} %bitcast.179) | data formatting | bytes 4194304 | tf_op jit(solution)/shard_map/jit(_take)/gather | solution.py:51
  69.8 7.4 gather.10
  78.1 160.3 %all-gather.7.cloned.1.call-done = f32[512,32,16]{1,2,0:T(8,128)} async-done(((f32[1,32,16]{1,2,0:T(8,128)}), f32[512,32,16]{1,2,0:T(8,128)}) %all-gather.7.cloned.1.call-update) | async-done | bytes 1048592 | tf_op jit(solution)/shard_map/all_gather | solution.py:59
  238.4 5.5 copy.96
  243.9 3.5 reshape.156
  247.4 3.3 fusion.10
  253.9 3.2 collective-permute-start.4
  258.4 3.4 collective-permute-start.6
  263.7 3.6 collective-permute-done.7
  272.4 4.3 collective-permute-start.8
  278.0 2.1 collective-permute-start.10
  280.2 2.2 collective-permute-start.11
  282.4 3.4 collective-permute-done.11
  287.6 106.4 %all-reduce.2 = (f32[16]{0:T(128)S(1)}, f32[16]{0:T(128)S(1)}) all-reduce(f32[16]{0:T(128)S(1)} %get-tuple-element.13, f32[16]{0:T(128)S(1)} %get-tuple-element.12), channel_id=1, replica_groups=mesh['gx'=32,'gy'=16] {'gx','gy'}, use_global_device_ids=true, to_apply=%region_2.4 | all-reduce | flops 32 | bytes 256 | tf_op jit(solution)/shard_map/psum | solution.py:85
  395.6 193.8 %all-gather.9.cloned.1.call-done = f32[512,32,16]{1,2,0:T(8,128)} async-done(((f32[1,32,16]{1,2,0:T(8,128)}), f32[512,32,16]{1,2,0:T(8,128)}) %all-gather.9.cloned.1.call-update) | async-done | bytes 1048592 | tf_op jit(solution)/shard_map/all_gather | solution.py:59
  589.5 5.6 copy.103
  595.0 3.7 reshape.158
  598.7 3.3 fusion.8
  604.3 3.0 collective-permute-start.12
  608.6 3.6 collective-permute-start.14
  612.2 1.9 collective-permute-start.15
  614.1 3.6 collective-permute-done.15
  622.7 4.3 collective-permute-start.16
  628.4 2.2 collective-permute-start.18
  630.5 2.2 collective-permute-start.19
  632.7 3.4 collective-permute-done.19
  638.0 106.4 %all-reduce.1 = (f32[16]{0:T(128)S(1)}, f32[16]{0:T(128)S(1)}) all-reduce(f32[16]{0:T(128)S(1)} %get-tuple-element.11, f32[16]{0:T(128)S(1)} %get-tuple-element.10), channel_id=1, replica_groups=mesh['gx'=32,'gy'=16] {'gx','gy'}, use_global_device_ids=true, to_apply=%region_6.8 | all-reduce | flops 32 | bytes 256 | tf_op jit(solution)/shard_map/psum | solution.py:85
  745.3 193.9 %all-gather.11.cloned.1.call-done = f32[512,32,16]{1,2,0:T(8,128)} async-done(((f32[1,32,16]{1,2,0:T(8,128)}), f32[512,32,16]{1,2,0:T(8,128)}) %all-gather.11.cloned.1.call-update) | async-done | bytes 1048592 | tf_op jit(solution)/shard_map/all_gather | solution.py:59
  939.2 5.6 copy.108
  944.8 3.5 reshape.160
  948.3 3.3 fusion.6
  954.7 3.0 collective-permute-start.20
  959.3 3.6 collective-permute-start.22
  962.9 1.9 collective-permute-start.23
  964.8 3.6 collective-permute-done.23
  973.5 4.3 collective-permute-start.24
  979.1 2.1 collective-permute-start.26
  981.2 2.2 collective-permute-start.27
  983.4 3.4 collective-permute-done.27
  988.7 106.4 %all-reduce = (f32[16]{0:T(128)S(1)}, f32[16]{0:T(128)S(1)}) all-reduce(f32[16]{0:T(128)S(1)} %get-tuple-element.9, f32[16]{0:T(128)S(1)} %get-tuple-element.8), channel_id=1, replica_groups=mesh['gx'=32,'gy'=16] {'gx','gy'}, use_global_device_ids=true, to_apply=%region_10.12 | all-reduce | flops 32 | bytes 256 | tf_op jit(solution)/shard_map/psum | solution.py:85
  (188 shorter events, 50.3 us)
Async XLA Ops:
  6.5 262.6 %copy-start = (f32[1,1,768,768]{3,2,1,0:T(8,128)S(1)}, f32[1,1,768,768]{3,2,1,0:T(8,128)}, u32[]{:S(2)}) copy-start(f32[1,1,768,768]{3,2,1,0:T(8,128)} %param.8) | copy-start | bytes 7077892
  6.5 25.1 %copy-start.17 = (f32[1,1,16,768]{3,2,1,0:T(8,128)S(1)}, f32[1,1,16,768]{3,2,1,0:T(8,128)}, u32[]{:S(2)}) copy-start(f32[1,1,16,768]{3,2,1,0:T(8,128)} %param.10) | copy-start | bytes 147460
  6.5 25.2 %copy-start.1 = (f32[1,1,32,768]{3,2,1,0:T(8,128)S(1)}, f32[1,1,32,768]{3,2,1,0:T(8,128)}, u32[]{:S(2)}) copy-start(f32[1,1,32,768]{3,2,1,0:T(8,128)} %param.9) | copy-start | bytes 294916
  6.5 231.9 %all-gather.7.cloned.1.call-start = ((), (), s32[]{:S(2)}) async-start(), calls=%async_computation | async-start | bytes 4202496 | tf_op jit(solution)/shard_map/all_gather | solution.py:59
  11.8 15.5 %copy-start.12 = (s32[1024]{0:T(1024)}, s32[1024]{0:T(1024)S(1)}, u32[]{:S(2)}) copy-start(s32[1024]{0:T(1024)S(1)} %pad_clamp_fusion.2) | copy-start | bytes 12292
  14.6 15.3 %collective-permute-start = (f32[1,16,256]{1,2,0:T(8,128)S(1)}, f32[1,16,256]{1,2,0:T(8,128)S(1)}, u32[]{:S(2)}, u32[]{:S(2)}) collective-permute-start(f32[1,16,256]{1,2,0:T(8,128)S(1)} %get-tuple-element.46), channel_id=1, source_target_pairs={{0,1},{1,2},{2,3},{3,4},{4,5},{5,6},{6,7},{7,8},{8,9},{9,10},{10,1... | collective-permute-start | bytes 49160 | tf_op jit(solution)/shard_map/ppermute | solution.py:18
  19.0 11.0 collective-permute-start.1
  20.3 7.1 collective-permute-start.2
  24.3 5.6 collective-permute-start.3
  32.5 556.9 %all-gather.9.cloned.1.call-start = ((), (), s32[]{:S(2)}) async-start(), calls=%async_computation.1 | async-start | bytes 4202496 | tf_op jit(solution)/shard_map/all_gather | solution.py:59
  250.8 16.7 %copy-start.9 = (s32[1024]{0:T(1024)S(1)}, s32[1024]{0:T(1024)}, u32[]{:S(2)}) copy-start(s32[1024]{0:T(1024)} %copy-done.8) | copy-start | bytes 12292
  250.8 18.4 %copy-start.19 = (pred[768]{0:T(1024)(128)(4,1)S(1)}, pred[768]{0:T(1024)(128)(4,1)}, u32[]{:S(2)}) copy-start(pred[768]{0:T(1024)(128)(4,1)} %copy-done.18) | copy-start | bytes 2308
  253.9 13.5 %collective-permute-start.4 = (f32[1,16,256]{1,2,0:T(8,128)S(1)}, f32[1,16,256]{1,2,0:T(8,128)S(1)}, u32[]{:S(2)}, u32[]{:S(2)}) collective-permute-start(f32[1,16,256]{1,2,0:T(8,128)S(1)} %get-tuple-element.42), channel_id=1, source_target_pairs={{0,1},{1,2},{2,3},{3,4},{4,5},{5,6},{6,7},{7,8},{8,9},{9,10},{10,1... | collective-permute-start | bytes 49160 | tf_op jit(solution)/shard_map/ppermute | solution.py:18
  257.0 10.3 collective-permute-start.5
  258.4 5.4 collective-permute-start.6
  261.8 5.6 collective-permute-start.7
  272.4 13.4 %collective-permute-start.8 = (f32[1,16,256]{1,2,0:T(8,128)S(1)}, f32[1,16,256]{1,2,0:T(8,128)S(1)}, u32[]{:S(2)}, u32[]{:S(2)}) collective-permute-start(f32[1,16,256]{1,2,0:T(8,128)S(1)} %get-tuple-element.38), channel_id=1, source_target_pairs={{0,1},{1,2},{2,3},{3,4},{4,5},{5,6},{6,7},{7,8},{8,9},{9,10},{10,1... | collective-permute-start | bytes 49160 | tf_op jit(solution)/shard_map/ppermute | solution.py:18
  276.7 9.1 collective-permute-start.9
  278.0 4.3 collective-permute-start.10
  280.2 5.6 collective-permute-start.11
  394.1 195.4 %copy-start.27 = (f32[16]{0:T(128)}, f32[16]{0:T(128)S(1)}, u32[]{:S(2)}) copy-start(f32[16]{0:T(128)S(1)} %add_divide_fusion.2) | copy-start | bytes 196
  395.6 543.6 %all-gather.11.cloned.1.call-start = ((), (), s32[]{:S(2)}) async-start(), calls=%async_computation.2 | async-start | bytes 4202496 | tf_op jit(solution)/shard_map/all_gather | solution.py:59
  602.1 15.7 %copy-start.10 = (s32[1024]{0:T(1024)S(1)}, s32[1024]{0:T(1024)}, u32[]{:S(2)}) copy-start(s32[1024]{0:T(1024)} %copy-done.8) | copy-start | bytes 12292
  602.1 17.5 %copy-start.3 = (f32[16,768]{1,0:T(8,128)S(1)}, f32[16,768]{1,0:T(8,128)}, u32[]{:S(2)}) copy-start(f32[16,768]{1,0:T(8,128)} %copy-done.2) | copy-start | bytes 147460
  602.1 17.4 %copy-start.20 = (pred[768]{0:T(1024)(128)(4,1)S(1)}, pred[768]{0:T(1024)(128)(4,1)}, u32[]{:S(2)}) copy-start(pred[768]{0:T(1024)(128)(4,1)} %copy-done.18) | copy-start | bytes 2308
  604.3 13.5 %collective-permute-start.12 = (f32[1,16,256]{1,2,0:T(8,128)S(1)}, f32[1,16,256]{1,2,0:T(8,128)S(1)}, u32[]{:S(2)}, u32[]{:S(2)}) collective-permute-start(f32[1,16,256]{1,2,0:T(8,128)S(1)} %get-tuple-element.34), channel_id=1, source_target_pairs={{0,1},{1,2},{2,3},{3,4},{4,5},{5,6},{6,7},{7,8},{8,9},{9,10},{10,1... | collective-permute-start | bytes 49160 | tf_op jit(solution)/shard_map/ppermute | solution.py:18
  607.3 10.5 collective-permute-start.13
  608.6 5.5 collective-permute-start.14
  612.2 5.6 collective-permute-start.15
  622.7 13.4 %collective-permute-start.16 = (f32[1,16,256]{1,2,0:T(8,128)S(1)}, f32[1,16,256]{1,2,0:T(8,128)S(1)}, u32[]{:S(2)}, u32[]{:S(2)}) collective-permute-start(f32[1,16,256]{1,2,0:T(8,128)S(1)} %get-tuple-element.30), channel_id=1, source_target_pairs={{0,1},{1,2},{2,3},{3,4},{4,5},{5,6},{6,7},{7,8},{8,9},{9,10},{10,1... | collective-permute-start | bytes 49160 | tf_op jit(solution)/shard_map/ppermute | solution.py:18
  627.0 9.1 collective-permute-start.17
  628.4 4.3 collective-permute-start.18
  630.5 5.6 collective-permute-start.19
  744.4 194.8 %copy-start.29 = (f32[16]{0:T(128)}, f32[16]{0:T(128)S(1)}, u32[]{:S(2)}) copy-start(f32[16]{0:T(128)S(1)} %add_divide_fusion.1) | copy-start | bytes 196
  951.6 16.9 %copy-start.11 = (s32[1024]{0:T(1024)S(1)}, s32[1024]{0:T(1024)}, u32[]{:S(2)}) copy-start(s32[1024]{0:T(1024)} %copy-done.8) | copy-start | bytes 12292
  951.8 18.4 %copy-start.21 = (pred[768]{0:T(1024)(128)(4,1)S(1)}, pred[768]{0:T(1024)(128)(4,1)}, u32[]{:S(2)}) copy-start(pred[768]{0:T(1024)(128)(4,1)} %copy-done.18) | copy-start | bytes 2308
  954.7 13.8 %collective-permute-start.20 = (f32[1,16,256]{1,2,0:T(8,128)S(1)}, f32[1,16,256]{1,2,0:T(8,128)S(1)}, u32[]{:S(2)}, u32[]{:S(2)}) collective-permute-start(f32[1,16,256]{1,2,0:T(8,128)S(1)} %get-tuple-element.26), channel_id=1, source_target_pairs={{0,1},{1,2},{2,3},{3,4},{4,5},{5,6},{6,7},{7,8},{8,9},{9,10},{10,1... | collective-permute-start | bytes 49160 | tf_op jit(solution)/shard_map/ppermute | solution.py:18
  957.8 10.7 collective-permute-start.21
  959.3 5.5 collective-permute-start.22
  962.9 5.6 collective-permute-start.23
  971.5 123.7 %copy-start.5 = (f32[16,768]{1,0:T(8,128)S(1)}, f32[16,768]{1,0:T(8,128)}, u32[]{:S(2)}) copy-start(f32[16,768]{1,0:T(8,128)} %copy-done.4) | copy-start | bytes 147460
  971.5 123.7 %copy-start.7 = (f32[16,768]{1,0:T(8,128)S(1)}, f32[16,768]{1,0:T(8,128)}, u32[]{:S(2)}) copy-start(f32[16,768]{1,0:T(8,128)} %copy-done.6) | copy-start | bytes 147460
  971.5 123.7 %copy-start.28 = (f32[16]{0:T(128)S(1)}, f32[16]{0:T(128)}, u32[]{:S(2)}) copy-start(f32[16]{0:T(128)} %copy-done.27) | copy-start | bytes 196
  971.5 123.7 %copy-start.30 = (f32[16]{0:T(128)S(1)}, f32[16]{0:T(128)}, u32[]{:S(2)}) copy-start(f32[16]{0:T(128)} %copy-done.29) | copy-start | bytes 196
  973.5 13.3 %collective-permute-start.24 = (f32[1,16,256]{1,2,0:T(8,128)S(1)}, f32[1,16,256]{1,2,0:T(8,128)S(1)}, u32[]{:S(2)}, u32[]{:S(2)}) collective-permute-start(f32[1,16,256]{1,2,0:T(8,128)S(1)} %get-tuple-element.22), channel_id=1, source_target_pairs={{0,1},{1,2},{2,3},{3,4},{4,5},{5,6},{6,7},{7,8},{8,9},{9,10},{10,1... | collective-permute-start | bytes 49160 | tf_op jit(solution)/shard_map/ppermute | solution.py:18
  977.8 9.1 collective-permute-start.25
  979.1 4.3 collective-permute-start.26
  981.2 5.6 collective-permute-start.27
  (14 other events, 84.6 us)
Sparse Core Ops, SparseCore 0:
  32.7 205.7 all-gather.6
  395.7 193.6 all-gather.8
  745.5 193.7 all-gather.10
where the time goes:
time: 1110 us; the launch traced here: 1100 us
  waiting for transfers between devices  572 us (52%)
  blocking collectives  319 us (29%)
  local copies, waits for them, and re-layouts  99.1 us (9%)
  starting transfers between devices  72 us (6%)
  matrix products  16.6 us (1%)
  between operations  14.7 us (1%)
    all_gather x3, waiting for transfers between devices, per_device(): lax.all_gather(lax.dot_general(residual, local_basis, (((1,), (1,)), ((),...  548 us
    psum x3, blocking collectives, per_device(): lax.psum((jnp.sum(residual * applied, axis=1), jnp.sum(applied * applied,...  319 us
    ppermute x14, starting transfers between devices, padded(): lax.ppermute(lax.slice_in_dim(block, block.shape[dim] - width, None, axis...  47.4 us
    gather x3, local copies, waits for them, and re-layouts, per_device(): jnp.take(coarse_inverse.reshape(mode_count, domain_count, mode_count), co...  26.6 us
    ppermute x14, starting transfers between devices, padded(): lax.ppermute(lax.slice_in_dim(block, 0, width, axis=dim), axis, backward)  24.5 us
    ppermute x14, waiting for transfers between devices, padded(): lax.ppermute(lax.slice_in_dim(block, 0, width, axis=dim), axis, backward)  23.7 us
  transfers between devices with their start and end apart: 31, of which 10 were waited for; matrix products, arithmetic and copies ran while one was open for 4% of the time, Pallas kernels for 0%

commit v1 on v0

--- a/solution.py
+++ b/solution.py
@@ -56,17 +56,25 @@
     solution = jnp.zeros_like(residual)
     for iteration in range(ITERS):
         lifted = lax.dot_general(
-            lax.all_gather(
-                lax.dot_general(
-                    residual,
-                    local_basis,
-                    (((1,), (1,)), ((), ())),
-                    precision=highest,
-                    preferred_element_type=jnp.float32,
+            jnp.concatenate(
+                lax.all_to_all(
+                    jnp.stack(
+                        [
+                            lax.dot_general(
+                                residual,
+                                local_basis,
+                                (((1,), (1,)), ((), ())),
+                                precision=highest,
+                                preferred_element_type=jnp.float32,
+                            )
+                        ]
+                        * lax.axis_size(("gx", "gy"))
+                    ),
+                    ("gx", "gy"),
+                    0,
+                    0,
                 ),
-                ("gx", "gy"),
                 axis=1,
-                tiled=True,
             ),
             reordered,
             (((1,), (1,)), ((), ())),

time: 1110 us -> 737 us (0.66)
  waiting for transfers between devices: 572 us -> 27.5 us
  blocking collectives: 319 us -> 453 us
  starting transfers between devices: 72 us -> 107 us
  other arithmetic: 9.34 us -> 29.9 us
  between operations: 14.7 us -> 1.31 us
    all_gather x3 -> x0, waiting for transfers between devices: 548 us -> none  [per_device(): lax.all_gather(lax.dot_general(residual, local_basis, (((1,), (1,)), ((),...]
    all_to_all x0 -> x2, blocking collectives: none -> 142 us  [per_device(): lax.all_to_all(jnp.stack([lax.dot_general(residual, local_basis, (((1,),...]
    ppermute x14, waiting for transfers between devices: 23.7 us -> 1.12 us  [padded(): lax.ppermute(lax.slice_in_dim(block, 0, width, axis=dim), axis, backward)]
    all_to_all x0 -> x1, starting transfers between devices: none -> 22.5 us  [per_device(): lax.all_to_all(jnp.stack([lax.dot_general(residual, local_basis, (((1,),...]
    gather x3 -> x1, local copies, waits for them, and re-layouts: 26.6 us -> 7.86 us  [per_device(): jnp.take(coarse_inverse.reshape(mode_count, domain_count, mode_count), co...]
    all_to_all x0 -> x1, waiting for transfers between devices: none -> 17.8 us  [per_device(): lax.all_to_all(jnp.stack([lax.dot_general(residual, local_basis, (((1,),...]
    all_gather x3 -> x0, local copies, waits for them, and re-layouts: 16.6 us -> none  [per_device(): lax.all_gather(lax.dot_general(residual, local_basis, (((1,), (1,)), ((),...]
    all_to_all x0 -> x3, other arithmetic: none -> 13.1 us  [per_device(): lax.all_to_all(jnp.stack([lax.dot_general(residual, local_basis, (((1,),...]
  transfers between devices with their start and end apart: 31 -> 29, of which waited for: 10 -> 9; matrix products, arithmetic and copies ran while one was open for 4% -> 5% of each run, Pallas kernels for 0% -> 0%
where the time goes in v1:
time: 737 us; the launch traced here: 731 us
  blocking collectives  453 us (61%)
  starting transfers between devices  107 us (15%)
  local copies, waits for them, and re-layouts  97.1 us (13%)
  other arithmetic  29.9 us (4%)
  waiting for transfers between devices  27.5 us (4%)
  matrix products  14.7 us (2%)
    psum x3, blocking collectives, per_device(): lax.psum((jnp.sum(residual * applied, axis=1), jnp.sum(applied * applied,...  312 us
    all_to_all x2, blocking collectives, per_device(): lax.all_to_all(jnp.stack([lax.dot_general(residual, local_basis, (((1,),...  142 us
    ppermute x14, starting transfers between devices, padded(): lax.ppermute(lax.slice_in_dim(block, block.shape[dim] - width, None, axis...  49.7 us
    ppermute x14, starting transfers between devices, padded(): lax.ppermute(lax.slice_in_dim(block, 0, width, axis=dim), axis, backward)  34.9 us
    all_to_all x1, starting transfers between devices, per_device(): lax.all_to_all(jnp.stack([lax.dot_general(residual, local_basis, (((1,),...  22.5 us
    unnamed x68, local copies, waits for them, and re-layouts  21.9 us
    reshape x2, local copies, waits for them, and re-layouts, per_device(): coarse_inverse.reshape(mode_count, domain_count, mode_count)  17.9 us
    all_to_all x1, waiting for transfers between devices, per_device(): lax.all_to_all(jnp.stack([lax.dot_general(residual, local_basis, (((1,),...  17.8 us
  transfers between devices with their start and end apart: 29, of which 9 were waited for; matrix products, arithmetic and copies ran while one was open for 5% of the time, Pallas kernels for 0%

profile of v1, /device:TPU:1, one launch (start us, length us, event | category | flops | bytes accessed | tf_op | source)
XLA Modules:
  0.0 731.0 jit_solution(11007985685335491376)
XLA Ops:
  0.9 4.4 sort.17
  8.0 8.7 %collective-permute-start.3 = (f32[1,16,128]{1,2,0:T(8,128)S(1)}, f32[1,16,128]{1,2,0:T(8,128)S(1)}, u32[]{:S(2)}, u32[]{:S(2)}) collective-permute-start(f32[1,16,128]{1,2,0:T(8,128)S(1)} %get-tuple-element.49), channel_id=1, source_target_pairs={{16,0},{32,16},{48,32},{64,48},{80,64},{96,80},{112,96},{128,112},... | collective-permute-start | bytes 24584 | tf_op jit(solution)/shard_map/ppermute | solution.py:21
  20.0 4.0 collective-permute-start
  27.9 2.3 stack.66
  30.2 4.6 reshape.206
  34.8 22.5 %all-to-all-start = ((f32[512,1,512]{2,1,0:T(1,128)}), f32[512,1,512]{2,1,0:T(1,128)S(1)}, u32[]{:S(2)}, u32[]{:S(2)}) async-start(f32[512,1,512]{2,1,0:T(1,128)} %reshape.206), calls=%async_computation | async-start | bytes 2097152 | tf_op jit(solution)/shard_map/all_to_all | solution.py:60
  57.4 6.4 reshape.36
  63.7 11.5 %copy.210 = f32[32,512,32]{2,0,1:T(8,128)} copy(f32[32,512,32]{2,1,0:T(8,128)} %reshape.36) | data formatting | bytes 4194304 | tf_op jit(solution)/shard_map/reshape | solution.py:52
  75.9 7.9 %gather_fusion = f32[512,32,32]{2,1,0:T(8,128)} fusion(f32[32,512,32]{2,0,1:T(8,128)} %copy.210, s32[1024]{0:T(1024)} %pad_clamp_fusion), kind=kCustom, calls=%fused_computation.14 | custom fusion | bytes 4196352 | tf_op jit(solution)/shard_map/jit(_take)/gather | solution.py:51
  84.4 6.3 select_bitcast_fusion
  90.7 6.7 copy.211
  97.3 17.8 %all-to-all-done = f32[512,1,512]{2,1,0:T(1,128)S(1)} async-done(((f32[512,1,512]{2,1,0:T(1,128)}), f32[512,1,512]{2,1,0:T(1,128)S(1)}, u32[]{:S(2)}, u32[]{:S(2)}) %all-to-all-start) | async-done | bytes 1048608 | tf_op jit(solution)/shard_map/all_to_all | solution.py:60
  116.6 4.4 reduce.1
  121.0 2.5 reshape.207
  123.5 3.4 copy.209
  127.0 3.3 convolution_bitcast_fusion.2
  134.7 4.0 collective-permute-start.4
  138.7 3.4 collective-permute-start.7
  151.9 4.0 collective-permute-start.8
  155.9 2.3 collective-permute-start.11
  158.3 4.4 collective-permute-start.10
  165.9 103.9 %all-reduce.2 = (f32[16]{0:T(128)S(1)}, f32[16]{0:T(128)S(1)}) all-reduce(f32[16]{0:T(128)S(1)} %get-tuple-element.13, f32[16]{0:T(128)S(1)} %get-tuple-element.12), channel_id=1, replica_groups=mesh['gx'=32,'gy'=16] {'gx','gy'}, use_global_device_ids=true, to_apply=%region_2.4 | all-reduce | flops 32 | bytes 256 | tf_op jit(solution)/shard_map/psum | solution.py:93
  270.7 2.2 stack.75
  273.0 3.8 reshape.208
  276.8 71.1 %all_to_all.15 = f32[512,1,512]{2,1,0:T(1,128)} all-to-all(f32[512,1,512]{2,1,0:T(1,128)S(1)} %reshape.208), channel_id=1, replica_groups=mesh['gx'=32,'gy'=16] {'gx','gy'}, dimensions={0} | all-to-all | bytes 2097152 | tf_op jit(solution)/shard_map/all_to_all | solution.py:60
  347.9 4.4 reduce.2
  352.3 2.5 reshape.209
  354.8 3.2 copy.216
  358.0 3.3 convolution_bitcast_fusion.1
  364.9 4.0 collective-permute-start.12
  368.9 3.4 collective-permute-start.15
  382.0 4.0 collective-permute-start.16
  386.1 2.3 collective-permute-start.19
  388.4 4.5 collective-permute-start.18
  396.0 103.9 %all-reduce.1 = (f32[16]{0:T(128)S(1)}, f32[16]{0:T(128)S(1)}) all-reduce(f32[16]{0:T(128)S(1)} %get-tuple-element.11, f32[16]{0:T(128)S(1)} %get-tuple-element.10), channel_id=1, replica_groups=mesh['gx'=32,'gy'=16] {'gx','gy'}, use_global_device_ids=true, to_apply=%region_6.8 | all-reduce | flops 32 | bytes 256 | tf_op jit(solution)/shard_map/psum | solution.py:93
  500.5 2.2 stack.84
  502.7 3.8 reshape.210
  506.5 70.6 %all_to_all.16 = f32[512,1,512]{2,1,0:T(1,128)} all-to-all(f32[512,1,512]{2,1,0:T(1,128)S(1)} %reshape.210), channel_id=1, replica_groups=mesh['gx'=32,'gy'=16] {'gx','gy'}, dimensions={0} | all-to-all | bytes 2097152 | tf_op jit(solution)/shard_map/all_to_all | solution.py:60
  577.1 4.4 reduce.3
  581.5 2.5 reshape.211
  584.0 3.2 copy.222
  587.2 3.3 convolution_bitcast_fusion
  595.0 4.0 collective-permute-start.20
  599.0 3.4 collective-permute-start.23
  612.2 4.0 collective-permute-start.24
  616.2 2.3 collective-permute-start.27
  618.5 4.4 collective-permute-start.26
  626.2 103.9 %all-reduce = (f32[16]{0:T(128)S(1)}, f32[16]{0:T(128)S(1)}) all-reduce(f32[16]{0:T(128)S(1)} %get-tuple-element.9, f32[16]{0:T(128)S(1)} %get-tuple-element.8), channel_id=1, replica_groups=mesh['gx'=32,'gy'=16] {'gx','gy'}, use_global_device_ids=true, to_apply=%region_10.12 | all-reduce | flops 32 | bytes 256 | tf_op jit(solution)/shard_map/psum | solution.py:93
  (191 shorter events, 66.3 us)
Async XLA Ops:
  0.0 147.4 %copy-start = (f32[1,1,768,768]{3,2,1,0:T(8,128)S(1)}, f32[1,1,768,768]{3,2,1,0:T(8,128)}, u32[]{:S(2)}) copy-start(f32[1,1,768,768]{3,2,1,0:T(8,128)} %param.8) | copy-start | bytes 7077892
  0.0 27.7 %copy-start.17 = (f32[1,1,16,768]{3,2,1,0:T(8,128)S(1)}, f32[1,1,16,768]{3,2,1,0:T(8,128)}, u32[]{:S(2)}) copy-start(f32[1,1,16,768]{3,2,1,0:T(8,128)} %param.10) | copy-start | bytes 147460
  0.0 27.7 %copy-start.2 = (f32[1,1,32,768]{3,2,1,0:T(8,128)S(1)}, f32[1,1,32,768]{3,2,1,0:T(8,128)}, u32[]{:S(2)}) copy-start(f32[1,1,32,768]{3,2,1,0:T(8,128)} %param.9) | copy-start | bytes 294916
  5.3 13.5 %copy-start.22 = (pred[768]{0:T(1024)(128)(4,1)}, pred[768]{0:T(1024)(128)(4,1)S(1)}, u32[]{:S(2)}) copy-start(pred[768]{0:T(1024)(128)(4,1)S(1)} %compare_and_fusion.1) | copy-start | bytes 2308
  6.2 17.8 %copy-start.13 = (s32[1024]{0:T(1024)}, s32[1024]{0:T(1024)S(1)}, u32[]{:S(2)}) copy-start(s32[1024]{0:T(1024)S(1)} %pad_clamp_fusion.2) | copy-start | bytes 12292
  8.0 16.1 %collective-permute-start.3 = (f32[1,16,128]{1,2,0:T(8,128)S(1)}, f32[1,16,128]{1,2,0:T(8,128)S(1)}, u32[]{:S(2)}, u32[]{:S(2)}) collective-permute-start(f32[1,16,128]{1,2,0:T(8,128)S(1)} %get-tuple-element.49), channel_id=1, source_target_pairs={{16,0},{32,16},{48,32},{64,48},{80,64},{96,80},{112,96},{128,112},... | collective-permute-start | bytes 24584 | tf_op jit(solution)/shard_map/ppermute | solution.py:21
  16.8 7.3 %collective-permute-start.2 = (f32[1,16,128]{1,2,0:T(8,128)S(1)}, f32[1,16,128]{1,2,0:T(8,128)S(1)}, u32[]{:S(2)}, u32[]{:S(2)}) collective-permute-start(f32[1,16,128]{1,2,0:T(8,128)S(1)} %get-tuple-element.48), channel_id=1, source_target_pairs={{0,16},{16,32},{32,48},{48,64},{64,80},{80,96},{96,112},{112,128},... | collective-permute-start | bytes 24584 | tf_op jit(solution)/shard_map/ppermute | solution.py:18
  18.7 6.5 collective-permute-start.1
  20.0 5.9 collective-permute-start
  34.8 80.3 %all-to-all-start = ((f32[512,1,512]{2,1,0:T(1,128)}), f32[512,1,512]{2,1,0:T(1,128)S(1)}, u32[]{:S(2)}, u32[]{:S(2)}) async-start(f32[512,1,512]{2,1,0:T(1,128)} %reshape.206), calls=%async_computation | async-start | bytes 2097152 | tf_op jit(solution)/shard_map/all_to_all | solution.py:60
  63.7 11.5 %copy-start.26 = (s32[512]{0:T(512)S(1)}, s32[512]{0:T(512)}, u32[]{:S(2)}) copy-start(s32[512]{0:T(512)} %param.13) | copy-start | bytes 6148
  130.3 15.4 %copy-start.10 = (s32[1024]{0:T(1024)S(1)}, s32[1024]{0:T(1024)}, u32[]{:S(2)}) copy-start(s32[1024]{0:T(1024)} %copy-done.9) | copy-start | bytes 12292
  130.3 17.1 %copy-start.19 = (pred[768]{0:T(1024)(128)(4,1)S(1)}, pred[768]{0:T(1024)(128)(4,1)}, u32[]{:S(2)}) copy-start(pred[768]{0:T(1024)(128)(4,1)} %copy-done.18) | copy-start | bytes 2308
  133.4 12.2 %collective-permute-start.5 = (f32[1,16,256]{1,2,0:T(8,128)S(1)}, f32[1,16,256]{1,2,0:T(8,128)S(1)}, u32[]{:S(2)}, u32[]{:S(2)}) collective-permute-start(f32[1,16,256]{1,2,0:T(8,128)S(1)} %get-tuple-element.43), channel_id=1, source_target_pairs={{1,0},{2,1},{3,2},{4,3},{5,4},{6,5},{7,6},{8,7},{9,8},{10,9},{11,1... | collective-permute-start | bytes 49160 | tf_op jit(solution)/shard_map/ppermute | solution.py:21
  134.7 10.9 %collective-permute-start.4 = (f32[1,16,256]{1,2,0:T(8,128)S(1)}, f32[1,16,256]{1,2,0:T(8,128)S(1)}, u32[]{:S(2)}, u32[]{:S(2)}) collective-permute-start(f32[1,16,256]{1,2,0:T(8,128)S(1)} %get-tuple-element.42), channel_id=1, source_target_pairs={{0,1},{1,2},{2,3},{3,4},{4,5},{5,6},{6,7},{7,8},{8,9},{9,10},{10,1... | collective-permute-start | bytes 49160 | tf_op jit(solution)/shard_map/ppermute | solution.py:18
  138.7 5.6 collective-permute-start.7
  142.1 3.4 collective-permute-start.6
  147.4 8.5 %copy-start.5 = (f32[16,768]{1,0:T(8,128)}, f32[16,768]{1,0:T(8,128)S(1)}, u32[]{:S(2)}) copy-start(f32[16,768]{1,0:T(8,128)S(1)} %fusion.23) | copy-start | bytes 147460
  150.6 13.4 %collective-permute-start.9 = (f32[1,16,256]{1,2,0:T(8,128)S(1)}, f32[1,16,256]{1,2,0:T(8,128)S(1)}, u32[]{:S(2)}, u32[]{:S(2)}) collective-permute-start(f32[1,16,256]{1,2,0:T(8,128)S(1)} %get-tuple-element.39), channel_id=1, source_target_pairs={{1,0},{2,1},{3,2},{4,3},{5,4},{6,5},{7,6},{8,7},{9,8},{10,9},{11,1... | collective-permute-start | bytes 49160 | tf_op jit(solution)/shard_map/ppermute | solution.py:21
  151.9 12.1 %collective-permute-start.8 = (f32[1,16,256]{1,2,0:T(8,128)S(1)}, f32[1,16,256]{1,2,0:T(8,128)S(1)}, u32[]{:S(2)}, u32[]{:S(2)}) collective-permute-start(f32[1,16,256]{1,2,0:T(8,128)S(1)} %get-tuple-element.38), channel_id=1, source_target_pairs={{0,1},{1,2},{2,3},{3,4},{4,5},{5,6},{6,7},{7,8},{8,9},{9,10},{10,1... | collective-permute-start | bytes 49160 | tf_op jit(solution)/shard_map/ppermute | solution.py:18
  155.9 6.8 collective-permute-start.11
  158.3 5.7 collective-permute-start.10
  361.4 14.4 %copy-start.11 = (s32[1024]{0:T(1024)S(1)}, s32[1024]{0:T(1024)}, u32[]{:S(2)}) copy-start(s32[1024]{0:T(1024)} %copy-done.9) | copy-start | bytes 12292
  361.4 16.2 %copy-start.4 = (f32[16,768]{1,0:T(8,128)S(1)}, f32[16,768]{1,0:T(8,128)}, u32[]{:S(2)}) copy-start(f32[16,768]{1,0:T(8,128)} %copy-done.3) | copy-start | bytes 147460
  361.4 16.1 %copy-start.20 = (pred[768]{0:T(1024)(128)(4,1)S(1)}, pred[768]{0:T(1024)(128)(4,1)}, u32[]{:S(2)}) copy-start(pred[768]{0:T(1024)(128)(4,1)} %copy-done.18) | copy-start | bytes 2308
  363.6 12.2 %collective-permute-start.13 = (f32[1,16,256]{1,2,0:T(8,128)S(1)}, f32[1,16,256]{1,2,0:T(8,128)S(1)}, u32[]{:S(2)}, u32[]{:S(2)}) collective-permute-start(f32[1,16,256]{1,2,0:T(8,128)S(1)} %get-tuple-element.35), channel_id=1, source_target_pairs={{1,0},{2,1},{3,2},{4,3},{5,4},{6,5},{7,6},{8,7},{9,8},{10,9},{11,1... | collective-permute-start | bytes 49160 | tf_op jit(solution)/shard_map/ppermute | solution.py:21
  364.9 10.9 %collective-permute-start.12 = (f32[1,16,256]{1,2,0:T(8,128)S(1)}, f32[1,16,256]{1,2,0:T(8,128)S(1)}, u32[]{:S(2)}, u32[]{:S(2)}) collective-permute-start(f32[1,16,256]{1,2,0:T(8,128)S(1)} %get-tuple-element.34), channel_id=1, source_target_pairs={{0,1},{1,2},{2,3},{3,4},{4,5},{5,6},{6,7},{7,8},{8,9},{9,10},{10,1... | collective-permute-start | bytes 49160 | tf_op jit(solution)/shard_map/ppermute | solution.py:18
  368.9 5.6 collective-permute-start.15
  372.3 3.5 collective-permute-start.14
  377.6 8.5 %copy-start.7 = (f32[16,768]{1,0:T(8,128)}, f32[16,768]{1,0:T(8,128)S(1)}, u32[]{:S(2)}) copy-start(f32[16,768]{1,0:T(8,128)S(1)} %fusion.22) | copy-start | bytes 147460
  380.7 13.4 %collective-permute-start.17 = (f32[1,16,256]{1,2,0:T(8,128)S(1)}, f32[1,16,256]{1,2,0:T(8,128)S(1)}, u32[]{:S(2)}, u32[]{:S(2)}) collective-permute-start(f32[1,16,256]{1,2,0:T(8,128)S(1)} %get-tuple-element.31), channel_id=1, source_target_pairs={{1,0},{2,1},{3,2},{4,3},{5,4},{6,5},{7,6},{8,7},{9,8},{10,9},{11,1... | collective-permute-start | bytes 49160 | tf_op jit(solution)/shard_map/ppermute | solution.py:21
  382.0 12.1 %collective-permute-start.16 = (f32[1,16,256]{1,2,0:T(8,128)S(1)}, f32[1,16,256]{1,2,0:T(8,128)S(1)}, u32[]{:S(2)}, u32[]{:S(2)}) collective-permute-start(f32[1,16,256]{1,2,0:T(8,128)S(1)} %get-tuple-element.30), channel_id=1, source_target_pairs={{0,1},{1,2},{2,3},{3,4},{4,5},{5,6},{6,7},{7,8},{8,9},{9,10},{10,1... | collective-permute-start | bytes 49160 | tf_op jit(solution)/shard_map/ppermute | solution.py:18
  386.1 6.8 collective-permute-start.19
  388.4 5.8 collective-permute-start.18
  590.5 15.4 %copy-start.12 = (s32[1024]{0:T(1024)S(1)}, s32[1024]{0:T(1024)}, u32[]{:S(2)}) copy-start(s32[1024]{0:T(1024)} %copy-done.9) | copy-start | bytes 12292
  590.7 16.9 %copy-start.21 = (pred[768]{0:T(1024)(128)(4,1)S(1)}, pred[768]{0:T(1024)(128)(4,1)}, u32[]{:S(2)}) copy-start(pred[768]{0:T(1024)(128)(4,1)} %copy-done.18) | copy-start | bytes 2308
  593.7 12.2 %collective-permute-start.21 = (f32[1,16,256]{1,2,0:T(8,128)S(1)}, f32[1,16,256]{1,2,0:T(8,128)S(1)}, u32[]{:S(2)}, u32[]{:S(2)}) collective-permute-start(f32[1,16,256]{1,2,0:T(8,128)S(1)} %get-tuple-element.27), channel_id=1, source_target_pairs={{1,0},{2,1},{3,2},{4,3},{5,4},{6,5},{7,6},{8,7},{9,8},{10,9},{11,1... | collective-permute-start | bytes 49160 | tf_op jit(solution)/shard_map/ppermute | solution.py:21
  595.0 10.9 %collective-permute-start.20 = (f32[1,16,256]{1,2,0:T(8,128)S(1)}, f32[1,16,256]{1,2,0:T(8,128)S(1)}, u32[]{:S(2)}, u32[]{:S(2)}) collective-permute-start(f32[1,16,256]{1,2,0:T(8,128)S(1)} %get-tuple-element.26), channel_id=1, source_target_pairs={{0,1},{1,2},{2,3},{3,4},{4,5},{5,6},{6,7},{7,8},{8,9},{9,10},{10,1... | collective-permute-start | bytes 49160 | tf_op jit(solution)/shard_map/ppermute | solution.py:18
  599.0 5.6 collective-permute-start.23
  602.4 3.4 collective-permute-start.22
  608.9 121.2 %copy-start.6 = (f32[16,768]{1,0:T(8,128)S(1)}, f32[16,768]{1,0:T(8,128)}, u32[]{:S(2)}) copy-start(f32[16,768]{1,0:T(8,128)} %copy-done.5) | copy-start | bytes 147460
  608.9 121.2 %copy-start.8 = (f32[16,768]{1,0:T(8,128)S(1)}, f32[16,768]{1,0:T(8,128)}, u32[]{:S(2)}) copy-start(f32[16,768]{1,0:T(8,128)} %copy-done.7) | copy-start | bytes 147460
  608.9 121.2 %copy-start.28 = (f32[16]{0:T(128)S(1)}, f32[16]{0:T(128)}, u32[]{:S(2)}) copy-start(f32[16]{0:T(128)} %copy-done.27) | copy-start | bytes 196
  608.9 121.2 %copy-start.30 = (f32[16]{0:T(128)S(1)}, f32[16]{0:T(128)}, u32[]{:S(2)}) copy-start(f32[16]{0:T(128)} %copy-done.29) | copy-start | bytes 196
  610.9 13.4 %collective-permute-start.25 = (f32[1,16,256]{1,2,0:T(8,128)S(1)}, f32[1,16,256]{1,2,0:T(8,128)S(1)}, u32[]{:S(2)}, u32[]{:S(2)}) collective-permute-start(f32[1,16,256]{1,2,0:T(8,128)S(1)} %get-tuple-element.23), channel_id=1, source_target_pairs={{1,0},{2,1},{3,2},{4,3},{5,4},{6,5},{7,6},{8,7},{9,8},{10,9},{11,1... | collective-permute-start | bytes 49160 | tf_op jit(solution)/shard_map/ppermute | solution.py:21
  612.2 12.1 %collective-permute-start.24 = (f32[1,16,256]{1,2,0:T(8,128)S(1)}, f32[1,16,256]{1,2,0:T(8,128)S(1)}, u32[]{:S(2)}, u32[]{:S(2)}) collective-permute-start(f32[1,16,256]{1,2,0:T(8,128)S(1)} %get-tuple-element.22), channel_id=1, source_target_pairs={{0,1},{1,2},{2,3},{3,4},{4,5},{5,6},{6,7},{7,8},{8,9},{9,10},{10,1... | collective-permute-start | bytes 49160 | tf_op jit(solution)/shard_map/ppermute | solution.py:18
  616.2 6.8 collective-permute-start.27
  618.5 5.7 collective-permute-start.26
  (12 other events, 40.2 us)
